TPU v7x, 32 devices: a whole 2x2x4 slice. The times are simulated.
32 devices in a mesh: fold: 2 (over y), vox: 16 (over z, x, core).
Axes of the slice: x: 2, y: 2, z: 4, core: 2. Of those that a mesh axis runs over, the one named last changes fastest.
Arguments:
- volumes: float32 [1024, 12288], P('fold', 'vox'), parts along dimension 0, may hold values from -6 to 6
- record_index: int32 [512], P('fold'), parts along dimension 0, may hold values from 0 to 511
- fold_of: int32 [1024], P('fold'), parts along dimension 0, may hold values from 0 to 4
- held_out: int32 [2], P('fold'), parts along dimension 0, may hold values from 0 to 4
- dictionary: float32 [12288, 512], P('vox'), may hold values from -1 to 1
Outputs:
- new_dictionary: float32 [24576, 512], P(('fold', 'vox')), parts along dimension 0
- code_matrix: float32 [512, 512], P('fold'), parts along dimension 0
- dict_gram: float32 [1024, 512], P('fold'), parts along dimension 0
There are 2 independent parts, one for each index of `fold`. A program takes and returns all parts, laid end to end along the dimension named above; an argument that names none is the same for every part. Nothing has to cross between parts.
All inputs are finite; a program needn't handle non-finite values.
Results may differ from a plain program's by a relative error of at most 0.0001.
Values sent between devices are 32-bit elements; how exact they have to be, the bound alone decides.
A program may use at most 64 MiB of HBM per device.

v0:
```python
import jax
import jax.numpy as jnp
from jax import lax
from jax.sharding import PartitionSpec as P

ISTA_STEPS = 5


penalty = 0.5


def matmul(left, right):
    return jnp.dot(left, right, precision=lax.Precision.HIGHEST, preferred_element_type=jnp.float32)


def inner_cross(left, right):
    return lax.dot_general(
        left,
        right,
        (((0,), (0,)), ((), ())),
        precision=lax.Precision.HIGHEST,
        preferred_element_type=jnp.float32,
    )


def row_bound(matrix):
    return jnp.max(jnp.sum(jnp.abs(matrix), axis=1))


def shrink_codes(correlation, gram_total):
    bound = row_bound(gram_total)
    limit = penalty / bound
    code_rows = jnp.zeros_like(correlation)
    for sweep in range(ISTA_STEPS):
        moved = code_rows - (matmul(code_rows, gram_total) - correlation) / bound
        code_rows = moved - jnp.clip(moved, -limit, limit)
    return code_rows


def shards(volumes, record_index, fold_of, held_out, dictionary):
    batch_rows = volumes[record_index]
    weight = (fold_of[record_index] != held_out[0]).astype(jnp.float32)
    corr_part = matmul(batch_rows, dictionary)
    gram_part = inner_cross(dictionary, dictionary)
    correlation, gram_total = lax.psum((corr_part, gram_part), "vox")
    code_rows = shrink_codes(correlation, gram_total)
    weighted = code_rows * weight[:, None]
    moment = inner_cross(code_rows, weighted)
    target = inner_cross(batch_rows, weighted)
    step_size = 1.0 / (1.0 + row_bound(moment))
    current = dictionary
    stepped = current - step_size * (matmul(current, moment) - target)
    squares = lax.psum(jnp.sum(stepped * stepped, axis=0), "vox")
    current = stepped / jnp.maximum(jnp.sqrt(squares), 1.0)
    stepped = current - step_size * (matmul(current, moment) - target)
    raw_gram = lax.psum(inner_cross(stepped, stepped), "vox")
    divisor = jnp.maximum(jnp.sqrt(jnp.diagonal(raw_gram)), 1.0)
    current = stepped / divisor
    dict_gram = raw_gram / (divisor[:, None] * divisor[None, :])
    return (current, code_rows, dict_gram)


def solution(mesh):
    in_specs = (P("fold", "vox"), P("fold"), P("fold"), P("fold"), P("vox", None))
    out_specs = (P(("fold", "vox"), None), P("fold", None), P("fold", None))
    return jax.shard_map(shards, mesh=mesh, in_specs=in_specs, out_specs=out_specs, check_vma=False)
```

profile of v0, /device:TPU:0, one launch (start us, length us, event | category | flops | bytes accessed | tf_op | source)
XLA Modules:
  0.0 297.6 jit_solution(10499714131739453914)
XLA Ops:
  7.2 0.0 copy-start
  7.2 0.0 all-reduce.6.cloned.1.call-start
  7.2 0.8 compare_select_fusion
  8.0 5.5 %fusion.42 = f32[512,512]{1,0:T(8,128)} fusion(f32[768,512]{1,0:T(8,128)} %param.9), kind=kOutput, calls=%fused_computation.64 | convolution fusion | flops 2415919104 | bytes 2621440 | tf_op jit(solution)/shard_map/dot_general | solution.py:17
  13.5 0.0 copy-done
  13.5 0.0 copy-start.2
  13.5 2.0 gather_fusion
  15.5 0.0 copy-done.2
  15.5 3.4 %fusion.43 = f32[256,512]{1,0:T(8,128)} fusion(f32[256,768]{1,0:T(8,128)} %gather_fusion, f32[768,512]{1,0:T(8,128)S(1)} %copy-done.2), kind=kOutput, calls=%fused_computation.65 | convolution fusion | flops 1207959552 | bytes 2883584 | tf_op jit(solution)/shard_map/dot_general | solution.py:13
  18.9 0.0 all-reduce.6.cloned.1.call-update
  19.0 0.0 copy-start.1
  19.0 0.0 all-reduce.4.cloned.1.call-start
  19.0 1.6 copy.14
  20.6 0.0 copy-done.1
  20.6 2.1 gather_fusion.1
  23.4 94.5 %all-reduce.6.cloned.1.call-done = (f32[256,512]{1,0:T(8,128)}, f32[512,512]{1,0:T(8,128)}) async-done(((f32[256,512]{1,0:T(8,128)}, f32[512,512]{1,0:T(8,128)}), (f32[256,512]{1,0:T(8,128)}, f32[512,512]{1,0:T(8,128)})) %all-reduce.6.cloned.1.call-update) | async-done | bytes 1572880 | tf_op jit(solution)/shard_map/psum | solution.py:45
  117.9 1.4 abs_reduce_fusion.1
  119.3 0.6 reduce_max.18
  119.9 3.8 %fusion.4 = f32[256,512]{1,0:T(8,128)} fusion(f32[256,512]{1,0:T(8,128)} %get-tuple-element.9, f32[512,512]{1,0:T(8,128)} %get-tuple-element.10, f32[]{:T(128)} %reduce_max.18), kind=kOutput, calls=%fused_computation.15 | convolution fusion | flops 805699584 | bytes 2097156 | tf_op jit(solution)/shard_map/dot_general | solution.py:13
  124.4 0.0 copy-start.6
  124.4 0.0 copy-start.7
  124.4 3.6 %fusion.6 = f32[256,512]{1,0:T(8,128)S(1)} fusion(f32[256,512]{1,0:T(8,128)} %get-tuple-element.9, f32[512,512]{1,0:T(8,128)} %get-tuple-element.10, f32[256,512]{1,0:T(8,128)} %fusion.4, f32[]{:T(128)S(6)} %neg.2, f32[]{:T(128)S(6)} %div.49, f32[]{:T(128)} %reduce_max.18), kind=kOutput, calls=%fused_computation.17 | convolution fusion | flops 806486016 | bytes 2621452 | tf_op jit(solution)/shard_map/dot_general | solution.py:13
  128.0 0.0 copy-done.6
  128.0 0.0 copy-done.7
  128.0 1.8 fusion.8
  129.8 1.8 fusion.10
  131.6 0.0 copy-start.4
  131.6 1.9 minimum_subtract_fusion
  133.5 0.0 copy-done.4
  133.5 0.0 copy-start.5
  133.5 2.7 fusion.14
  136.2 2.1 abs_reduce_fusion
  138.3 0.0 copy-done.5
  138.3 0.6 reduce_max.19
  139.6 6.2 %multiply_reduce_fusion = (f32[512]{0:T(512)S(1)}, f32[768,512]{0,1:T(8,128)}) fusion(f32[768,512]{0,1:T(8,128)} %copy.14, f32[768,512]{0,1:T(8,128)} %fusion.14, f32[512,512]{0,1:T(8,128)} %get-tuple-element.12, f32[768,512]{1,0:T(8,128)S(1)} %copy-done.2, f32[]{:T(128)S(6)} %div.54), kind=kOutput, calls=%fused_computation.7 | convolution fusion | flops 2417884672 | bytes 7342084 | tf_op jit(solution)/shard_map/dot_general | solution.py:13
  145.7 30.2 %psum.30 = f32[512]{0:T(512)S(1)} all-reduce(f32[512]{0:T(512)S(1)} %get-tuple-element.13), channel_id=1, replica_groups=mesh['fold'=2,'vox'=16] {'vox'}, use_global_device_ids=true, to_apply=%region_7.8 | all-reduce | flops 512 | bytes 4096 | tf_op jit(solution)/shard_map/psum | solution.py:53
  175.9 5.7 %multiply_subtract_fusion = f32[768,512]{0,1:T(8,128)S(1)} fusion(f32[768,512]{0,1:T(8,128)} %fusion.14, f32[512,512]{0,1:T(8,128)} %get-tuple-element.12, f32[768,512]{0,1:T(8,128)} %get-tuple-element.14, f32[512]{0:T(512)S(1)} %sqrt_maximum_fusion.1, f32[]{:T(128)S(6)} %div.54), kind=kOutput, calls=%fused_computation.6 | convolution fusion | flops 2417885184 | bytes 5769220 | tf_op jit(solution)/shard_map/dot_general | solution.py:13
  181.6 3.7 %fusion.44 = f32[512,512]{1,0:T(8,128)} fusion(f32[768,512]{0,1:T(8,128)S(1)} %multiply_subtract_fusion), kind=kOutput, calls=%fused_computation.66 | convolution fusion | flops 2415919104 | bytes 2621440 | tf_op jit(solution)/shard_map/dot_general | solution.py:17
  185.3 0.0 all-reduce.4.cloned.1.call-update
  185.3 91.0 %all-reduce.4.cloned.1.call-done = f32[512,512]{1,0:T(8,128)} async-done(((f32[512,512]{1,0:T(8,128)}), f32[512,512]{1,0:T(8,128)}) %all-reduce.4.cloned.1.call-update) | async-done | bytes 1048592 | tf_op jit(solution)/shard_map/psum | solution.py:56
  276.4 8.7 %gather_fusion.2 = f32[512]{0:T(512)S(1)} fusion(f32[512,512]{1,0:T(8,128)} %all-reduce.4.cloned.1.call-done, s32[512]{0:T(512)S(1)} %bitcast.25), kind=kCustom, calls=%fused_computation.2 | custom fusion | bytes 8192 | tf_op jit(solution)/shard_map/jit(diagonal)/cond/branch_0_fun/gather | solution.py:57
  285.1 1.3 broadcast_divide_fusion
  286.5 0.0 copy-start.3
  286.5 3.1 %copy.17 = f32[768,512]{1,0:T(8,128)} copy(f32[768,512]{0,1:T(8,128)} %broadcast_divide_fusion) | data formatting | bytes 3145728
  289.6 0.0 copy-done.3
  289.6 1.2 multiply_divide_fusion
  (5 shorter events, 0.0 us)
Async XLA Ops:
  7.2 6.4 %copy-start = (f32[512,768]{1,0:T(8,128)S(1)}, f32[512,768]{1,0:T(8,128)}, u32[]{:S(2)}) copy-start(f32[512,768]{1,0:T(8,128)} %param.5) | copy-start | bytes 4718596
  7.2 110.7 %all-reduce.6.cloned.1.call-start = ((), (), s32[]{:S(2)}) async-start(), calls=%async_computation.1 | async-start | bytes 3145728 | tf_op jit(solution)/shard_map/psum | solution.py:45
  13.5 2.0 copy-start.2
  19.0 1.7 copy-start.1
  19.0 257.4 %all-reduce.4.cloned.1.call-start = ((), (), s32[]{:S(2)}) async-start(), calls=%async_computation | async-start | bytes 2097152 | tf_op jit(solution)/shard_map/psum | solution.py:56
  124.4 3.6 %copy-start.6 = (f32[512,512]{1,0:T(8,128)S(1)}, f32[512,512]{1,0:T(8,128)}, u32[]{:S(2)}) copy-start(f32[512,512]{1,0:T(8,128)} %get-tuple-element.10) | copy-start | bytes 3145732
  124.4 3.6 %copy-start.7 = (f32[256,512]{1,0:T(8,128)S(1)}, f32[256,512]{1,0:T(8,128)}, u32[]{:S(2)}) copy-start(f32[256,512]{1,0:T(8,128)} %get-tuple-element.9) | copy-start | bytes 1572868
  131.6 1.9 copy-start.4
  133.5 4.8 %copy-start.5 = (f32[256,512]{1,0:T(8,128)}, f32[256,512]{1,0:T(8,128)S(1)}, u32[]{:S(2)}) copy-start(f32[256,512]{1,0:T(8,128)S(1)} %minimum_subtract_fusion) | copy-start | bytes 1572868
  286.5 3.1 %copy-start.3 = (f32[512,512]{1,0:T(8,128)S(1)}, f32[512,512]{1,0:T(8,128)}, u32[]{:S(2)}) copy-start(f32[512,512]{1,0:T(8,128)} %all-reduce.4.cloned.1.call-done) | copy-start | bytes 3145732
Sparse Core Ops, SparseCore 0:
  19.1 98.7 all-reduce.5
  185.4 90.8 all-reduce.3
where the time goes:
time: 298 us
  waiting for transfers between devices  186 us (62%)
  matrix products  42.1 us (14%)
  blocking collectives  30.2 us (10%)
  local copies, waits for them, and re-layouts  17.6 us (6%)
  between operations  16.2 us (5%)
  other arithmetic  5.95 us (2%)
    psum x1, waiting for transfers between devices, shards(): correlation, gram_total = lax.psum((corr_part, gram_part), 'vox')  94.5 us
    psum x1, waiting for transfers between devices, shards(): raw_gram = lax.psum(inner_cross(stepped, stepped), 'vox')  91 us
    psum x1, blocking collectives, shards(): squares = lax.psum(jnp.sum(stepped * stepped, axis=0), 'vox')  30.2 us
    dot_general x8, matrix products, matmul(): jnp.dot(left, right, precision=lax.Precision.HIGHEST, preferred_element_t...  28.1 us
    dot_general x4, matrix products, inner_cross(): lax.dot_general(left, right, (((0,), (0,)), ((), ())), precision=lax.Prec...  13.9 us
    gather x1, local copies, waits for them, and re-layouts, shards(): divisor = jnp.maximum(jnp.sqrt(jnp.diagonal(raw_gram)), 1.0)  8.74 us
  transfers between devices with their start and end apart: 2, of which 2 were waited for; matrix products, arithmetic and copies ran while one was open for 1% of the time, Pallas kernels for 0%

commit v1 on v0

v1 whole, which is shorter than its diff:
```python
import functools

import jax
import jax.numpy as jnp
from jax import lax
from jax.experimental import pallas as pl
from jax.experimental.pallas import tpu as pltpu
from jax.sharding import PartitionSpec as P

ISTA_STEPS = 5
PIECES = 3
LANES = 128

penalty = 0.5
MESH = pl.DeviceIdType.MESH


def dot(left, right, dims):
    return lax.dot_general(
        left, right, (dims, ((), ())), precision=lax.Precision.HIGH, preferred_element_type=jnp.float32
    )


def row_bound(matrix):
    return jnp.max(jnp.sum(jnp.abs(matrix), axis=1))


def reduce_kernel(n, x_ref, out_ref, got0, sum0, got1, sum1, got2, sem0, sem1, sem2, gat2, gat1, gat0):
    me = lax.axis_index("vox")
    low, mid, high = lax.rem(me, 2), lax.rem(me // 2, 2), me // 4
    peers = n // 4
    half, quarter = n // 2, n // 4
    mate0 = me + 1 - 2 * low
    mate1 = me + 2 - 4 * mid
    there = [lax.rem(high + step, peers) for step in range(1, peers)]
    back = [lax.rem(high + peers - step, peers) for step in range(1, peers)]
    place = low * half + mid * quarter
    own = place + high

    def device(z):
        return {"vox": z * 4 + mid * 2 + low}

    def copy(src, dst, sems, index, to):
        return pltpu.make_async_remote_copy(
            src_ref=src, dst_ref=dst, send_sem=sems.at[(0,) + index], recv_sem=sems.at[(1,) + index],
            device_id=to, device_id_type=MESH,
        )

    barrier = pltpu.get_barrier_semaphore()
    for to in [{"vox": mate0}, {"vox": mate1}] + [device(z) for z in there]:
        pl.semaphore_signal(barrier, inc=1, device_id=to, device_id_type=MESH)
    pl.semaphore_wait(barrier, 2 + len(there))

    sends = []
    first = []
    for k in range(PIECES):
        c = copy(x_ref.at[k, pl.ds((1 - low) * half, half)], got0.at[k], sem0, (k,), {"vox": mate0})
        c.start()
        first.append(c)
    second = []
    for k in range(PIECES):
        first[k].wait_recv()
        sum0[k] = x_ref[k, pl.ds(low * half, half)] + got0[k]
        c = copy(sum0.at[k, pl.ds((1 - mid) * quarter, quarter)], got1.at[k], sem1, (k,), {"vox": mate1})
        c.start()
        second.append(c)
    third = []
    for k in range(PIECES):
        second[k].wait_recv()
        sum1[k] = sum0[k, pl.ds(mid * quarter, quarter)] + got1[k]
        for step, z in enumerate(there):
            c = copy(sum1.at[k, z], got2.at[k, step], sem2, (k, step), device(z))
            c.start()
            third.append(c)
    for k in range(PIECES):
        total = sum1[k, high]
        for step in range(peers - 1):
            third[k * (peers - 1) + step].wait_recv()
            total = total + got2[k, step]
        out_ref[k, own] = total
        for step, z in enumerate(there):
            c = copy(out_ref.at[k, own], out_ref.at[k, own], gat2, (k, step), device(z))
            c.start()
            sends.append(c)
    for k in range(PIECES):
        for step, z in enumerate(back):
            spot = out_ref.at[k, place + z]
            copy(spot, spot, gat2, (k, step), device(z)).wait_recv()
        spot = out_ref.at[k, pl.ds(place, quarter)]
        c = copy(spot, spot, gat1, (k,), {"vox": mate1})
        c.start()
        sends.append(c)
    for k in range(PIECES):
        spot = out_ref.at[k, pl.ds(low * half + (1 - mid) * quarter, quarter)]
        copy(spot, spot, gat1, (k,), {"vox": mate1}).wait_recv()
        spot = out_ref.at[k, pl.ds(low * half, half)]
        c = copy(spot, spot, gat0, (k,), {"vox": mate0})
        c.start()
        sends.append(c)
    for k in range(PIECES):
        spot = out_ref.at[k, pl.ds((1 - low) * half, half)]
        copy(spot, spot, gat0, (k,), {"vox": mate0}).wait_recv()
    for c in first + second + third + sends:
        c.wait_send()


def all_sum(n, flat):
    rows = flat.shape[0]
    chunk = -(-rows // (PIECES * n * 8)) * 8
    padded = PIECES * n * chunk
    if padded != rows:
        flat = jnp.pad(flat, ((0, padded - rows), (0, 0)))
    peers = n // 4
    shape = (PIECES, n, chunk, LANES)
    sem = pltpu.SemaphoreType.DMA
    out = pl.pallas_call(
        functools.partial(reduce_kernel, n),
        out_shape=jax.ShapeDtypeStruct(shape, jnp.float32),
        in_specs=[pl.BlockSpec(memory_space=pltpu.VMEM)],
        out_specs=pl.BlockSpec(memory_space=pltpu.VMEM),
        scratch_shapes=[
            pltpu.VMEM((PIECES, n // 2, chunk, LANES), jnp.float32),
            pltpu.VMEM((PIECES, n // 2, chunk, LANES), jnp.float32),
            pltpu.VMEM((PIECES, n // 4, chunk, LANES), jnp.float32),
            pltpu.VMEM((PIECES, n // 4, chunk, LANES), jnp.float32),
            pltpu.VMEM((PIECES, peers, chunk, LANES), jnp.float32),
            sem((2, PIECES)), sem((2, PIECES)), sem((2, PIECES, peers)),
            sem((2, PIECES, peers)), sem((2, PIECES)), sem((2, PIECES)),
        ],
        compiler_params=pltpu.CompilerParams(collective_id=0, has_side_effects=True),
    )(flat.reshape(shape))
    return out.reshape(padded, LANES)[:rows]


def pairs(tiles):
    return [(i, j) for i in range(tiles) for j in range(i, tiles)]


def pack(matrix):
    tiles = matrix.shape[0] // LANES
    return jnp.concatenate(
        [matrix[i * LANES:(i + 1) * LANES, j * LANES:(j + 1) * LANES] for i, j in pairs(tiles)], axis=0
    )


def unpack(flat, tiles):
    where = {pair: k for k, pair in enumerate(pairs(tiles))}

    def tile(i, j):
        if i > j:
            return tile(j, i).T
        k = where[(i, j)]
        return flat[k * LANES:(k + 1) * LANES]

    return jnp.concatenate(
        [jnp.concatenate([tile(i, j) for j in range(tiles)], axis=1) for i in range(tiles)], axis=0
    )


def shards(n, volumes, record_index, fold_of, held_out, dictionary):
    atoms = dictionary.shape[1]
    batch_rows = volumes[record_index]
    weight = (fold_of[record_index] != held_out[0]).astype(jnp.float32)
    joint = jnp.concatenate([dictionary, batch_rows.T], axis=1)
    part = dot(joint, joint, ((0,), (0,)))
    whole = unpack(all_sum(n, pack(part)), part.shape[0] // LANES)
    gram, correlation = whole[:atoms, :atoms], whole[atoms:, :atoms]
    bound = row_bound(gram)
    limit = penalty / bound
    moved = correlation / bound
    codes = moved - jnp.clip(moved, -limit, limit)
    for sweep in range(ISTA_STEPS - 1):
        moved = codes - (dot(codes, gram, ((1,), (0,))) - correlation) / bound
        codes = moved - jnp.clip(moved, -limit, limit)
    weighted = codes * weight[:, None]
    moment = dot(codes, weighted, ((0,), (0,)))
    step_size = 1.0 / (1.0 + row_bound(moment))
    scaled = step_size * weighted
    shift = step_size * moment
    side = dot(whole[:, atoms:], scaled, ((1,), (0,)))
    image = whole[:, :atoms]
    image = image - dot(image, shift, ((1,), (0,))) + side
    top = jnp.eye(atoms, dtype=jnp.float32) - shift
    length = jnp.sum(top * image[:atoms], axis=0) + jnp.sum(scaled * image[atoms:], axis=0)
    divisor = jnp.maximum(jnp.sqrt(jnp.maximum(length, 0.0)), 1.0)
    both = jnp.concatenate([top, scaled, image], axis=0) / divisor
    both = both - dot(both, shift, ((1,), (0,)))
    size = whole.shape[0]
    mix = jnp.concatenate([both[:atoms], both[atoms:size] + scaled], axis=0)
    image = both[size:] + side
    raw_gram = dot(mix, image, ((0,), (0,)))
    divisor = jnp.maximum(jnp.sqrt(jnp.maximum(jnp.diagonal(raw_gram), 0.0)), 1.0)
    current = dot(joint, mix, ((1,), (0,))) / divisor
    dict_gram = raw_gram / (divisor[:, None] * divisor[None, :])
    return (current, codes, dict_gram)


def solution(mesh):
    in_specs = (P("fold", "vox"), P("fold"), P("fold"), P("fold"), P("vox", None))
    out_specs = (P(("fold", "vox"), None), P("fold", None), P("fold", None))
    return jax.shard_map(
        functools.partial(shards, mesh.shape["vox"]), mesh=mesh, in_specs=in_specs, out_specs=out_specs, check_vma=False
    )
```

time: 298 us -> 142 us (0.48)
  waiting for transfers between devices: 186 us -> 0 us
  local copies, waits for them, and re-layouts: 17.6 us -> 63.5 us
  Pallas kernels: 0 us -> 36.4 us
  blocking collectives: 30.2 us -> 0 us
  between operations: 16.2 us -> 3.29 us
  matrix products: 42.1 us -> 31.7 us
    psum x2 -> x0, waiting for transfers between devices: 186 us -> none  [the longest x1 94.5 us: shards(): correlation, gram_total = lax.psum((corr_part, gram_part), 'vox')]
    pallas_call x0 -> x1, Pallas kernels: none -> 36.4 us  [all_sum(): pl.pallas_call(functools.partial(reduce_kernel, n), out_shape=jax.ShapeDt...]
    unnamed x18 -> x79, local copies, waits for them, and re-layouts: 4.78 us -> 39.4 us
    psum x1 -> x0, blocking collectives: 30.2 us -> none  [shards(): squares = lax.psum(jnp.sum(stepped * stepped, axis=0), 'vox')]
    transpose x0 -> x11, local copies, waits for them, and re-layouts: none -> 13.3 us  [the longest x10 12.1 us: tile(): return tile(j, i).T]
    dot_general x12 -> x11, matrix products: 42.1 us -> 31.7 us  [dot(): lax.dot_general(left, right, (dims, ((), ())), precision=lax.Precision.HI...]
    gather x1, local copies, waits for them, and re-layouts: 8.74 us -> 4.52 us  [shards(): jnp.diagonal(raw_gram)]
    concatenate x0 -> x5, local copies, waits for them, and re-layouts: none -> 3.25 us  [the longest x3 2.52 us: unpack(): jnp.concatenate([tile(i, j) for j in range(tiles)], axis=1)]
  transfers between devices with their start and end apart: 2 -> 0, of which waited for: 2 -> 0; matrix products, arithmetic and copies ran while one was open for 1% -> 0% of each run, Pallas kernels for 0% -> 0%
where the time goes in v1:
time: 142 us; the launch traced here: 140 us
  local copies, waits for them, and re-layouts  63.5 us (45%)
  Pallas kernels  36.4 us (26%)
  matrix products  31.7 us (22%)
  other arithmetic  5.13 us (4%)
  between operations  3.29 us (2%)
    unnamed x79, local copies, waits for them, and re-layouts  39.4 us
    pallas_call x1, Pallas kernels, all_sum(): pl.pallas_call(functools.partial(reduce_kernel, n), out_shape=jax.ShapeDt...  36.4 us
    dot_general x11, matrix products, dot(): lax.dot_general(left, right, (dims, ((), ())), precision=lax.Precision.HI...  31.7 us
    transpose x10, local copies, waits for them, and re-layouts, tile(): return tile(j, i).T  12.1 us
    gather x1, local copies, waits for them, and re-layouts, shards(): jnp.diagonal(raw_gram)  4.52 us

profile of v1, /device:TPU:0, one launch (start us, length us, event | category | flops | bytes accessed | tf_op | source)
XLA Modules:
  0.0 140.0 jit_solution(8554575690226693949)
XLA Ops:
  2.1 2.0 %gather_fusion.1 = s32[256]{0:T(256)S(1)} fusion(s32[512]{0:T(512)} %param.7, s32[1024]{0:T(1024)S(1)} %pad_clamp_fusion), kind=kCustom, calls=%fused_computation.1 | custom fusion | bytes 3072 | tf_op jit(solution)/shard_map/gather | solution.py:163
  4.1 1.1 gather_fusion
  5.2 1.2 copy.26
  6.4 5.9 %fusion.5 = f32[768,768]{1,0:T(8,128)S(1)} fusion(f32[768,256]{1,0:T(8,128)} %copy.26, f32[768,512]{1,0:T(8,128)} %param.9), kind=kOutput, calls=%fused_computation.11 | convolution fusion | flops 2718498816 | bytes 4718592 | tf_op jit(solution)/shard_map/dot_general | solution.py:19
  12.6 1.1 copy-done.4
  13.7 36.4 %shard_map.76 = f32[3,16,56,128]{3,2,1,0:T(8,128)} custom-call(f32[3,16,56,128]{3,2,1,0:T(8,128)} %bitcast.63), custom_call_target="tpu_custom_call" | custom-call | tf_op jit(solution)/shard_map/pallas_call | solution.py:116
  50.1 1.5 %constant_dynamic-update-slice_fusion.43 = f32[128,768]{0,1:T(8,128)} fusion(f32[2688,128]{1,0:T(8,128)} %bitcast.43), kind=kLoop, calls=%fused_computation.122 | loop fusion | bytes 131072
  51.6 1.5 %constant_dynamic-update-slice_fusion.66 = f32[768,768]{1,0:T(8,128)} fusion(f32[2688,128]{1,0:T(8,128)} %bitcast.44), kind=kLoop, calls=%fused_computation.145 | loop fusion | bytes 131072
  53.1 1.5 %constant_dynamic-update-slice_fusion.65 = f32[768,768]{1,0:T(8,128)} fusion(f32[768,768]{1,0:T(8,128)} %constant_dynamic-update-slice_fusion.66, f32[2688,128]{1,0:T(8,128)} %bitcast.45), kind=kLoop, calls=%fused_computation.144 | loop fusion | bytes 131072
  54.5 1.6 %constant_dynamic-update-slice_fusion.64 = f32[768,768]{1,0:T(8,128)} fusion(f32[768,768]{1,0:T(8,128)} %constant_dynamic-update-slice_fusion.65, f32[2688,128]{1,0:T(8,128)} %bitcast.46), kind=kLoop, calls=%fused_computation.143 | loop fusion | bytes 131072
  56.1 1.5 %constant_dynamic-update-slice_fusion.63 = f32[768,768]{1,0:T(8,128)} fusion(f32[768,768]{1,0:T(8,128)} %constant_dynamic-update-slice_fusion.64, f32[2688,128]{1,0:T(8,128)} %bitcast.47), kind=kLoop, calls=%fused_computation.142 | loop fusion | bytes 131072
  57.6 1.5 %constant_dynamic-update-slice_fusion.62 = f32[768,768]{1,0:T(8,128)} fusion(f32[768,768]{1,0:T(8,128)} %constant_dynamic-update-slice_fusion.63, f32[2688,128]{1,0:T(8,128)} %bitcast.48), kind=kLoop, calls=%fused_computation.141 | loop fusion | bytes 131072
  59.0 1.7 %constant_dynamic-update-slice_fusion.61 = (f32[768,768]{1,0:T(8,128)}, f32[128,128]{0,1:T(8,128)S(1)}, f32[128,128]{1,0:T(8,128)S(1)}, f32[128,128]{1,0:T(8,128...) fusion(f32[768,768]{1,0:T(8,128)} %constant_dynamic-update-slice_fusion.62, ...), kind=kLoop, calls=%fused_computation.140 | loop fusion | bytes 917504
  61.1 0.7 copy.39
  65.1 1.2 copy.42
  66.3 0.8 constant_dynamic-update-slice_fusion.60
  67.1 1.5 %constant_dynamic-update-slice_fusion.59 = (f32[768,768]{1,0:T(8,128)}, f32[128,768]{1,0:T(8,128)}) fusion(f32[768,768]{1,0:T(8,128)} %constant_dynamic-update-slice_fusion.60, f32[128,128]{1,0:T(8,128)} %copy.39), kind=kLoop, calls=%fused_computation.138 | loop fusion | bytes 196608
  68.6 1.5 %bitcast_dynamic-update-slice_fusion.1 = (f32[768,768]{1,0:T(8,128)}, f32[128,768]{1,0:T(8,128)}) fusion(f32[768,768]{1,0:T(8,128)} %get-tuple-element.68, f32[128,128]{0,1:T(8,128)} %copy-done.5, f32[128,768]{1,0:T(8,128)} %get-tuple-element.69), kind=kLoop, calls=%fused_computation.147 | loop fusion | bytes 196608
  72.7 1.6 %copy.40 = f32[128,128]{1,0:T(8,128)} copy(f32[128,128]{0,1:T(8,128)} %get-tuple-element.30) | data formatting | bytes 131072 | tf_op jit(solution)/shard_map/transpose | solution.py:151
  74.2 1.6 %copy.41 = f32[128,128]{1,0:T(8,128)} copy(f32[128,128]{0,1:T(8,128)} %get-tuple-element.31) | data formatting | bytes 131072 | tf_op jit(solution)/shard_map/transpose | solution.py:151
  75.8 1.5 %constant_dynamic-update-slice_fusion.58 = (f32[768,768]{1,0:T(8,128)}, f32[128,768]{1,0:T(8,128)}) fusion(f32[768,768]{1,0:T(8,128)} %get-tuple-element.29, f32[128,128]{1,0:T(8,128)} %copy.40), kind=kLoop, calls=%fused_computation.137 | loop fusion | bytes 196608
  77.9 1.5 %constant_dynamic-update-slice_fusion.72 = (f32[768,768]{1,0:T(8,128)}, f32[128,768]{1,0:T(8,128)}) fusion(f32[768,768]{1,0:T(8,128)} %get-tuple-element.62, f32[128,128]{1,0:T(8,128)} %copy.41, f32[128,768]{1,0:T(8,128)} %get-tuple-element.63), kind=kLoop, calls=%fused_computation.175 | loop fusion | bytes 196608
  81.5 0.9 copy.30
  82.4 1.6 %copy.29 = f32[128,128]{1,0:T(8,128)} copy(f32[128,128]{0,1:T(8,128)} %get-tuple-element.25) | data formatting | bytes 131072 | tf_op jit(solution)/shard_map/transpose | solution.py:151
  84.0 1.6 %copy.28 = f32[128,128]{1,0:T(8,128)} copy(f32[128,128]{0,1:T(8,128)} %get-tuple-element.26) | data formatting | bytes 131072 | tf_op jit(solution)/shard_map/transpose | solution.py:151
  85.5 1.5 %constant_dynamic-update-slice_fusion.57 = (f32[768,768]{1,0:T(8,128)}, f32[128,768]{1,0:T(8,128)S(1)}) fusion(f32[768,768]{1,0:T(8,128)} %get-tuple-element.22, f32[128,128]{1,0:T(8,128)} %copy.28), kind=kLoop, calls=%fused_computation.136 | loop fusion | bytes 196608
  87.7 1.5 %constant_dynamic-update-slice_fusion.71 = (f32[768,768]{1,0:T(8,128)}, f32[128,768]{1,0:T(8,128)S(1)}) fusion(f32[768,768]{1,0:T(8,128)} %get-tuple-element.56, f32[128,128]{1,0:T(8,128)} %copy.29, f32[128,768]{1,0:T(8,128)S(1)} %get-tuple-element.57), kind=kLoop, calls=%fused_computation.174 | loop fusion | bytes 196608
  90.5 0.8 slice_dynamic-update-slice_fusion.7
  91.2 0.7 copy-done.8
  92.1 0.9 copy.34
  93.0 1.6 %copy.33 = f32[128,128]{1,0:T(8,128)} copy(f32[128,128]{0,1:T(8,128)} %get-tuple-element.16) | data formatting | bytes 131072 | tf_op jit(solution)/shard_map/transpose | solution.py:151
  94.6 1.6 %copy.32 = f32[128,128]{1,0:T(8,128)} copy(f32[128,128]{0,1:T(8,128)} %get-tuple-element.18) | data formatting | bytes 131072 | tf_op jit(solution)/shard_map/transpose | solution.py:151
  96.2 1.5 %constant_dynamic-update-slice_fusion.56 = (f32[768,768]{1,0:T(8,128)}, f32[128,768]{1,0:T(8,128)S(1)}, f32[128,768]{1,0:T(8,128)}) fusion(f32[768,768]{1,0:T(8,128)} %get-tuple-element.11, f32[128,128]{1,0:T(8,128)} %copy.32, f32[128,768]{1,0:T(8,128)} %get-tuple-element.13, f32[2688,128]{1,0:T(8,128)S(1)} %bitcast.59), kind=kLoop, calls=%fused_computation.135 | loop fusion | bytes 327680
  98.3 1.5 %constant_dynamic-update-slice_fusion.69 = (f32[768,768]{1,0:T(8,128)}, f32[128,768]{1,0:T(8,128)S(1)}) fusion(f32[768,768]{1,0:T(8,128)} %get-tuple-element.48, f32[128,128]{1,0:T(8,128)} %copy.33, f32[128,768]{1,0:T(8,128)S(1)} %get-tuple-element.49), kind=kLoop, calls=%fused_computation.172 | loop fusion | bytes 196608
  102.7 1.3 abs_reduce_fusion.1
  105.4 2.9 %fusion.13 = f32[256,512]{1,0:T(8,128)S(1)} fusion(f32[]{:T(128)S(6)} %neg.2, f32[]{:T(128)S(6)} %div.49, f32[]{:T(128)} %reduce_max.18, f32[128,768]{1,0:T(8,128)} %copy-done.6, f32[128,768]{1,0:T(8,128)} %get-tuple-element.10, f32[128,768]{1,0:T(8,128)} %get-tuple-element.41, f32[128,768]{1,0:T(8,128)} %get-tuple-element.40, f32[128,768]{1,0:T(8,128)S(1)} %copy.42, ...), kind=kOutput, calls=%fused_computation.24 | convolution fusion | flops 405143552 | bytes 2883596 | tf_op jit(solution)/shard_map/dot_general | solution.py:19
  108.4 2.5 %fusion.15 = f32[256,512]{1,0:T(8,128)S(1)} fusion(f32[256,512]{1,0:T(8,128)S(1)} %fusion.13, f32[]{:T(128)S(6)} %neg.2, f32[]{:T(128)S(6)} %div.49, f32[]{:T(128)} %reduce_max.18, f32[128,768]{1,0:T(8,128)S(1)} %copy-done.7, f32[128,768]{1,0:T(8,128)S(1)} %copy-done.9, f32[128,768]{1,0:T(8,128)} %get-tuple-element.41, f32[128,768]{1,0:T(8,128)} %get-tuple-element.40, ...), kind=kOutput, calls=%fused_computation.26 | convolution fusion | flops 404750336 | bytes 3407884 | tf_op jit(solution)/shard_map/dot_general | solution.py:19
  110.9 2.5 %fusion.17 = f32[256,512]{1,0:T(8,128)S(1)} fusion(f32[256,512]{1,0:T(8,128)S(1)} %fusion.15, f32[]{:T(128)S(6)} %neg.2, f32[]{:T(128)S(6)} %div.49, f32[]{:T(128)} %reduce_max.18, f32[128,768]{1,0:T(8,128)S(1)} %copy-done.7, f32[128,768]{1,0:T(8,128)S(1)} %copy-done.9, f32[128,768]{1,0:T(8,128)} %get-tuple-element.41, f32[128,768]{1,0:T(8,128)} %get-tuple-element.40, ...), kind=kOutput, calls=%fused_computation.28 | convolution fusion | flops 404750336 | bytes 3407884 | tf_op jit(solution)/shard_map/dot_general | solution.py:19
  113.3 2.5 %minimum_subtract_fusion = f32[256,512]{1,0:T(8,128)S(1)} fusion(f32[256,512]{1,0:T(8,128)S(1)} %fusion.17, f32[]{:T(128)S(6)} %neg.2, f32[]{:T(128)S(6)} %div.49, f32[]{:T(128)} %reduce_max.18, f32[128,768]{1,0:T(8,128)S(1)} %copy-done.7, f32[128,768]{1,0:T(8,128)S(1)} %copy-done.9, f32[128,768]{1,0:T(8,128)} %get-tuple-element.41, ...), kind=kOutput, calls=%fused_computation.55 | convolution fusion | flops 405143552 | bytes 3407884 | tf_op jit(solution)/shard_map/dot_general | solution.py:19
  115.9 0.8 abs_reduce_fusion
  118.1 1.9 %fusion.23 = f32[768,512]{1,0:T(8,128)S(1)} fusion(f32[256,512]{1,0:T(8,128)S(1)} %multiply_multiply_fusion, f32[768,768]{1,0:T(8,128)} %get-tuple-element.5), kind=kOutput, calls=%fused_computation.43 | convolution fusion | flops 603979776 | bytes 2883584 | tf_op jit(solution)/shard_map/dot_general | solution.py:19
  120.0 3.2 %fusion.9 = f32[768,512]{1,0:T(8,128)S(1)} fusion(f32[768,512]{1,0:T(8,128)S(1)} %fusion.23, f32[768,768]{1,0:T(8,128)} %get-tuple-element.5, f32[512,512]{1,0:T(8,128)S(1)} %get-tuple-element.71, f32[]{:T(128)S(6)} %div.54), kind=kOutput, calls=%fused_computation.18 | convolution fusion | flops 1209008128 | bytes 5767172 | tf_op jit(solution)/shard_map/dot_general | solution.py:19
  123.6 2.8 %convolution_subtract_fusion = f32[1536,512]{1,0:T(8,128)S(1)} fusion(f32[768,512]{1,0:T(8,128)S(1)} %fusion.9, f32[256,512]{1,0:T(8,128)S(1)} %multiply_multiply_fusion, f32[512,512]{1,0:T(8,128)S(1)} %get-tuple-element.4, f32[512]{0:T(512)S(1)} %sqrt_maximum_fusion.1, f32[512,512]{1,0:T(8,128)S(1)} %get-tuple-element.71, f32[]{:T(128)S(6)} %div.54), kind=kOutput, calls=%fused_computation.3 | convolution fusion | flops 2419326976 | bytes 7342084 | tf_op jit(solution)/shard_map/dot_general | solution.py:19
  126.7 1.0 copy-done.3
  127.6 1.5 %fusion.6 = f32[512,512]{1,0:T(8,128)S(1)} fusion(f32[768,512]{1,0:T(8,128)S(1)} %fusion.23, f32[1536,512]{1,0:T(8,128)S(1)} %convolution_subtract_fusion, f32[256,512]{1,0:T(8,128)S(1)} %slice_add_fusion.2, f32[512,512]{1,0:T(8,128)S(1)} %slice.270), kind=kOutput, calls=%fused_computation.14 | convolution fusion | flops 1208745984 | bytes 5767168 | tf_op jit(solution)/shard_map/dot_general | solution.py:19
  129.1 4.5 %gather_fusion.2 = f32[512]{0:T(512)S(1)} fusion(f32[512,512]{1,0:T(8,128)S(1)} %fusion.6, s32[512]{0:T(512)S(1)} %bitcast.42), kind=kCustom, calls=%fused_computation.2 | custom fusion | bytes 8192 | tf_op jit(solution)/shard_map/jit(diagonal)/cond/branch_0_fun/gather | solution.py:192
  133.7 5.1 %broadcast_divide_fusion = f32[768,512]{1,0:T(8,128)} fusion(f32[512]{0:T(512)S(1)} %sqrt_maximum_fusion, f32[256,512]{1,0:T(8,128)S(1)} %slice_add_fusion.2, f32[512,512]{1,0:T(8,128)} %copy-done.3, f32[768,256]{1,0:T(8,128)} %copy.26, f32[768,512]{1,0:T(8,128)} %param.9), kind=kOutput, calls=%fused_computation.45 | convolution fusion | flops 1813315584 | bytes 5507072 | tf_op jit(solution)/shard_map/dot_general | solution.py:19
  138.8 1.2 multiply_divide_fusion
  (77 shorter events, 17.4 us)
Async XLA Ops:
  0.6 3.5 %copy-start = (f32[512,768]{1,0:T(8,128)S(1)}, f32[512,768]{1,0:T(8,128)}, u32[]{:S(2)}) copy-start(f32[512,768]{1,0:T(8,128)} %param.5) | copy-start | bytes 4718596
  12.6 1.1 copy-start.4
  54.5 15.6 %copy-start.1 = (f32[3,16,56,128]{3,2,1,0:T(8,128)S(1)}, f32[3,16,56,128]{3,2,1,0:T(8,128)}, u32[]{:S(2)}) copy-start(f32[3,16,56,128]{3,2,1,0:T(8,128)} %shard_map.76) | copy-start | bytes 4128772
  60.8 3.7 %copy-start.5 = (f32[128,128]{0,1:T(8,128)}, f32[128,128]{0,1:T(8,128)S(1)}, u32[]{:S(2)}) copy-start(f32[128,128]{0,1:T(8,128)S(1)} %copy.47) | copy-start | bytes 196612
  91.2 0.7 copy-start.8
  101.8 0.9 copy-start.6
  105.4 3.0 %copy-start.7 = (f32[128,768]{1,0:T(8,128)S(1)}, f32[128,768]{1,0:T(8,128)}, u32[]{:S(2)}) copy-start(f32[128,768]{1,0:T(8,128)} %copy-done.6) | copy-start | bytes 1179652
  105.4 3.0 %copy-start.9 = (f32[128,768]{1,0:T(8,128)S(1)}, f32[128,768]{1,0:T(8,128)}, u32[]{:S(2)}) copy-start(f32[128,768]{1,0:T(8,128)} %get-tuple-element.10) | copy-start | bytes 1179652
  115.9 10.6 %copy-start.2 = (f32[256,512]{1,0:T(8,128)}, f32[256,512]{1,0:T(8,128)S(1)}, u32[]{:S(2)}) copy-start(f32[256,512]{1,0:T(8,128)S(1)} %minimum_subtract_fusion) | copy-start | bytes 1572868
  126.7 1.0 copy-start.3

commit v2 on v1

v2 whole, which is shorter than its diff:
```python
import functools

import jax
import jax.numpy as jnp
from jax import lax
from jax.experimental import pallas as pl
from jax.experimental.pallas import tpu as pltpu
from jax.sharding import PartitionSpec as P

ISTA_STEPS = 5
PIECES = 3
LANES = 128
STRIP = 256

penalty = 0.5
MESH = pl.DeviceIdType.MESH
ROWS = ((1,), (0,))
CROSS = ((0,), (0,))


def split(value):
    high = value.astype(jnp.bfloat16)
    return high, (value - high.astype(jnp.float32)).astype(jnp.bfloat16)


def dot(left, right, dims=ROWS):
    return lax.dot_general(left, right, (dims, ((), ())), preferred_element_type=jnp.float32)


def dot3(left, right, dims=ROWS):
    return dot(left[0], right[0], dims) + (dot(left[0], right[1], dims) + dot(left[1], right[0], dims))


def pairs(tiles):
    return [(i, j) for i in range(tiles) for j in range(i, tiles)]


def column_of(row):
    return jnp.broadcast_to(row, (LANES, row.shape[1])).T[:, :1]


def match(index_ref, records):
    column = column_of(index_ref[...])
    return lax.broadcasted_iota(jnp.int32, (column.shape[0], records), 1) == column


def reduce_kernel(
    n, chunk, index_ref, vol_ref, dict_ref, out_ref, high_out, low_out,
    joint_h, joint_l, turned_h, turned_l, x_ref, got0, sum0, got1, sum1, got2,
    sem0, sem1, sem2, gat2, gat1, gat0, keep,
):
    me = lax.axis_index("vox")
    low, mid, high = lax.rem(me, 2), lax.rem(me // 2, 2), me // 4
    peers = n // 4
    half, quarter = n // 2 * chunk, n // 4 * chunk
    mate0 = {"vox": me + 1 - 2 * low}
    mate1 = {"vox": me + 2 - 4 * mid}
    there = [lax.rem(high + step, peers) for step in range(1, peers)]
    back = [lax.rem(high + peers - step, peers) for step in range(1, peers)]

    def at(start, size):
        return pl.ds(pl.multiple_of(start, 8), size)

    place = low * half + mid * quarter
    own = at(place + high * chunk, chunk)

    def device(z):
        return {"vox": z * 4 + mid * 2 + low}

    def copy(src, dst, sems, index, to):
        return pltpu.make_async_remote_copy(
            src_ref=src, dst_ref=dst, send_sem=sems.at[(0,) + index], recv_sem=sems.at[(1,) + index],
            device_id=to, device_id_type=MESH,
        )

    barrier = pltpu.get_barrier_semaphore()
    for to in [mate0, mate1] + [device(z) for z in there]:
        pl.semaphore_signal(barrier, inc=1, device_id=to, device_id_type=MESH)

    atoms = dict_ref.shape[1]
    size = joint_h.shape[1]
    picked = jnp.where(match(index_ref, vol_ref.shape[0]), 1.0, 0.0).astype(jnp.bfloat16)
    for part, joint, turned in zip(split(vol_ref[...]), (joint_h, joint_l), (turned_h, turned_l)):
        rows = dot(picked, part).astype(jnp.bfloat16)
        turned[atoms:] = rows
        joint[:, atoms:] = rows.T
    for part, joint, turned in zip(split(dict_ref[...]), (joint_h, joint_l), (turned_h, turned_l)):
        joint[:, :atoms] = part
        turned[:atoms] = part.T
    saves = [
        pltpu.make_async_copy(joint_h, high_out, keep.at[0]),
        pltpu.make_async_copy(joint_l, low_out, keep.at[1]),
    ]
    for c in saves:
        c.start()

    tiles = size // LANES
    per_piece = n * chunk // LANES
    order = {pair: t for t, pair in enumerate(pairs(tiles))}
    for t in range(len(order), PIECES * per_piece):
        x_ref[t // per_piece, pl.ds(t % per_piece * LANES, LANES)] = jnp.zeros((LANES, LANES), jnp.float32)
    first = []

    def send_first(k):
        if k == 0:
            pl.semaphore_wait(barrier, 2 + len(there))
        c = copy(x_ref.at[k, at((1 - low) * half, half)], got0.at[k], sem0, (k,), mate0)
        c.start()
        first.append(c)

    done = 0
    for top in range(0, size, STRIP):
        strip = dot3(
            (turned_h[top:top + STRIP], turned_l[top:top + STRIP]), (joint_h[:, top:], joint_l[:, top:])
        )
        for i in range(top // LANES, (top + STRIP) // LANES):
            for j in range(i, tiles):
                t = order[(i, j)]
                x_ref[t // per_piece, pl.ds(t % per_piece * LANES, LANES)] = strip[
                    i * LANES - top:(i + 1) * LANES - top, j * LANES - top:(j + 1) * LANES - top
                ]
                done += 1
        while len(first) < PIECES and (done >= (len(first) + 1) * per_piece or done == len(order)):
            send_first(len(first))

    sends = []
    second = []
    for k in range(PIECES):
        first[k].wait_recv()
        sum0[k] = x_ref[k, at(low * half, half)] + got0[k]
        c = copy(sum0.at[k, at((1 - mid) * quarter, quarter)], got1.at[k], sem1, (k,), mate1)
        c.start()
        second.append(c)
    third = []
    for k in range(PIECES):
        second[k].wait_recv()
        sum1[k] = sum0[k, at(mid * quarter, quarter)] + got1[k]
        for step, z in enumerate(there):
            c = copy(sum1.at[k, at(z * chunk, chunk)], got2.at[k, step], sem2, (k, step), device(z))
            c.start()
            third.append(c)
    for k in range(PIECES):
        total = sum1[k, at(high * chunk, chunk)]
        for step in range(peers - 1):
            third[k * (peers - 1) + step].wait_recv()
            total = total + got2[k, step]
        out_ref[k, own] = total
        for step, z in enumerate(there):
            c = copy(out_ref.at[k, own], out_ref.at[k, own], gat2, (k, step), device(z))
            c.start()
            sends.append(c)
    for k in range(PIECES):
        for step, z in enumerate(back):
            spot = out_ref.at[k, at(place + z * chunk, chunk)]
            copy(spot, spot, gat2, (k, step), device(z)).wait_recv()
        spot = out_ref.at[k, at(place, quarter)]
        c = copy(spot, spot, gat1, (k,), mate1)
        c.start()
        sends.append(c)
    for k in range(PIECES):
        spot = out_ref.at[k, at(low * half + (1 - mid) * quarter, quarter)]
        copy(spot, spot, gat1, (k,), mate1).wait_recv()
        spot = out_ref.at[k, at(low * half, half)]
        c = copy(spot, spot, gat0, (k,), mate0)
        c.start()
        sends.append(c)
    for k in range(PIECES):
        spot = out_ref.at[k, at((1 - low) * half, half)]
        copy(spot, spot, gat0, (k,), mate0).wait_recv()
    for c in first + second + third + sends:
        c.wait_send()
    for c in saves:
        c.wait()


def joint_gram(n, record_index, volumes, dictionary):
    voxels, atoms = dictionary.shape
    size = atoms + record_index.shape[1]
    rows = len(pairs(size // LANES)) * LANES
    chunk = -(-rows // (PIECES * n * 8)) * 8
    peers = n // 4
    sem = pltpu.SemaphoreType.DMA
    vmem = pl.BlockSpec(memory_space=pltpu.VMEM)
    anywhere = pl.BlockSpec(memory_space=pl.ANY)
    return pl.pallas_call(
        functools.partial(reduce_kernel, n, chunk),
        out_shape=(
            jax.ShapeDtypeStruct((PIECES, n * chunk, LANES), jnp.float32),
            jax.ShapeDtypeStruct((voxels, size), jnp.bfloat16),
            jax.ShapeDtypeStruct((voxels, size), jnp.bfloat16),
        ),
        in_specs=[vmem] * 3,
        out_specs=(vmem, anywhere, anywhere),
        scratch_shapes=[
            pltpu.VMEM((voxels, size), jnp.bfloat16),
            pltpu.VMEM((voxels, size), jnp.bfloat16),
            pltpu.VMEM((size, voxels), jnp.bfloat16),
            pltpu.VMEM((size, voxels), jnp.bfloat16),
            pltpu.VMEM((PIECES, n * chunk, LANES), jnp.float32),
            pltpu.VMEM((PIECES, n // 2 * chunk, LANES), jnp.float32),
            pltpu.VMEM((PIECES, n // 2 * chunk, LANES), jnp.float32),
            pltpu.VMEM((PIECES, n // 4 * chunk, LANES), jnp.float32),
            pltpu.VMEM((PIECES, n // 4 * chunk, LANES), jnp.float32),
            pltpu.VMEM((PIECES, peers, chunk, LANES), jnp.float32),
            sem((2, PIECES)), sem((2, PIECES)), sem((2, PIECES, peers)),
            sem((2, PIECES, peers)), sem((2, PIECES)), sem((2, PIECES)),
            sem((2,)),
        ],
        compiler_params=pltpu.CompilerParams(collective_id=0, has_side_effects=True),
    )(record_index, volumes, dictionary)


def update_kernel(
    flat_ref, index_ref, fold_ref, held_ref, high_in, low_in, new_out, code_out, gram_out,
    full, full_h, full_l, joint_h, joint_l, both, side_ref, new_ref, code_ref, gram_ref, sems,
):
    size = full.shape[0]
    batch, atoms = code_ref.shape
    voxels = joint_h.shape[0]
    loads = [
        pltpu.make_async_copy(high_in, joint_h, sems.at[0]),
        pltpu.make_async_copy(low_in, joint_l, sems.at[1]),
    ]
    for c in loads:
        c.start()
    per_piece = flat_ref.shape[1] // LANES
    for t, (i, j) in enumerate(pairs(size // LANES)):
        tile = flat_ref[t // per_piece, pl.ds(t % per_piece * LANES, LANES)]
        spots = [(i, j, tile)] + ([(j, i, tile.T)] if j > i else [])
        for row, column, value in spots:
            where = (pl.ds(row * LANES, LANES), pl.ds(column * LANES, LANES))
            full[where] = value
            full_h[where], full_l[where] = split(value)
    bound = jnp.max(jnp.sum(jnp.abs(full[:atoms, :atoms]), axis=0))
    limit = penalty / bound
    gram = (full_h[:atoms, :atoms], full_l[:atoms, :atoms])
    correlation = full[atoms:, :atoms]
    moved = correlation / bound
    codes = moved - jnp.clip(moved, -limit, limit)
    for sweep in range(ISTA_STEPS - 1):
        moved = codes - (dot3(split(codes), gram) - correlation) / bound
        codes = moved - jnp.clip(moved, -limit, limit)
    code_ref[...] = codes
    stores = [pltpu.make_async_copy(code_ref, code_out, sems.at[2])]
    stores[0].start()
    folds = jnp.sum(jnp.where(match(index_ref, fold_ref.shape[1]), fold_ref[...], 0), axis=1, keepdims=True)
    weight = jnp.where(folds != held_ref[0], 1.0, 0.0)
    weighted = codes * weight
    moment = dot3(split(codes), split(weighted), CROSS)
    step_size = 1.0 / (1.0 + jnp.max(jnp.sum(jnp.abs(moment), axis=0)))
    scaled = step_size * weighted
    shift = step_size * moment
    shift_parts = split(shift)
    scaled_parts = split(scaled)
    side = dot3((full_h[:, atoms:], full_l[:, atoms:]), scaled_parts)
    side_ref[...] = side
    image = full[:, :atoms] - dot3((full_h[:, :atoms], full_l[:, :atoms]), shift_parts) + side
    both[size:] = image
    diagonal = lax.broadcasted_iota(jnp.int32, (atoms, atoms), 0) == lax.broadcasted_iota(
        jnp.int32, (atoms, atoms), 1
    )
    both[:atoms] = jnp.where(diagonal, 1.0, 0.0) - shift
    both[atoms:size] = scaled
    length = jnp.sum(both[:size] * both[size:], axis=0, keepdims=True)
    inverse = 1.0 / jnp.maximum(jnp.sqrt(jnp.maximum(length, 0.0)), 1.0)
    for top in range(0, 2 * size, STRIP):
        rows = pl.ds(top, STRIP)
        value = both[rows] * inverse
        value = value - dot3(split(value), shift_parts)
        if top >= size:
            value = value + side_ref[pl.ds(top - size, STRIP)]
        elif top >= atoms:
            value = value + scaled[top - atoms:top - atoms + STRIP]
        both[rows] = value
    length = jnp.sum(both[:size] * both[size:], axis=0, keepdims=True)
    inverse = 1.0 / jnp.maximum(jnp.sqrt(jnp.maximum(length, 0.0)), 1.0)
    mix = split(both[:size] * inverse)
    for c in loads:
        c.wait()
    for k, top in enumerate(range(0, voxels, STRIP)):
        rows = pl.ds(top, STRIP)
        new_ref[rows] = dot3((joint_h[rows], joint_l[rows]), mix)
        c = pltpu.make_async_copy(new_ref.at[rows], new_out.at[rows], sems.at[4 + k])
        c.start()
        stores.append(c)
    gram_ref[...] = dot3(mix, split(both[size:] * inverse), CROSS)
    c = pltpu.make_async_copy(gram_ref, gram_out, sems.at[3])
    c.start()
    stores.append(c)
    for c in stores:
        c.wait()


def update(flat, record_index, fold_of, held_out, joint_h, joint_l, atoms):
    voxels, size = joint_h.shape
    batch = record_index.shape[1]
    vmem = pl.BlockSpec(memory_space=pltpu.VMEM)
    anywhere = pl.BlockSpec(memory_space=pl.ANY)
    return pl.pallas_call(
        update_kernel,
        out_shape=(
            jax.ShapeDtypeStruct((voxels, atoms), jnp.float32),
            jax.ShapeDtypeStruct((batch, atoms), jnp.float32),
            jax.ShapeDtypeStruct((atoms, atoms), jnp.float32),
        ),
        in_specs=[vmem, vmem, vmem, pl.BlockSpec(memory_space=pltpu.SMEM), anywhere, anywhere],
        out_specs=(anywhere, anywhere, anywhere),
        scratch_shapes=[
            pltpu.VMEM((size, size), jnp.float32),
            pltpu.VMEM((size, size), jnp.bfloat16),
            pltpu.VMEM((size, size), jnp.bfloat16),
            pltpu.VMEM((voxels, size), jnp.bfloat16),
            pltpu.VMEM((voxels, size), jnp.bfloat16),
            pltpu.VMEM((2 * size, atoms), jnp.float32),
            pltpu.VMEM((size, atoms), jnp.float32),
            pltpu.VMEM((voxels, atoms), jnp.float32),
            pltpu.VMEM((batch, atoms), jnp.float32),
            pltpu.VMEM((atoms, atoms), jnp.float32),
            pltpu.SemaphoreType.DMA((4 + voxels // STRIP,)),
        ],
    )(flat, record_index, fold_of, held_out, joint_h, joint_l)


def shards(n, volumes, record_index, fold_of, held_out, dictionary):
    record_index = record_index.reshape(1, -1)
    flat, joint_h, joint_l = joint_gram(n, record_index, volumes, dictionary)
    return update(flat, record_index, fold_of.reshape(1, -1), held_out, joint_h, joint_l, dictionary.shape[1])


def solution(mesh):
    in_specs = (P("fold", "vox"), P("fold"), P("fold"), P("fold"), P("vox", None))
    out_specs = (P(("fold", "vox"), None), P("fold", None), P("fold", None))
    return jax.shard_map(
        functools.partial(shards, mesh.shape["vox"]), mesh=mesh, in_specs=in_specs, out_specs=out_specs, check_vma=False
    )
```

time: 142 us -> 54 us (0.38); the launches traced: 140 us -> 53.8 us
  local copies, waits for them, and re-layouts: 63.5 us -> 0 us
  matrix products: 31.7 us -> 0 us
  Pallas kernels: 36.4 us -> 52.5 us
  other arithmetic: 5.13 us -> 0 us
  between operations: 3.29 us -> 1.28 us
    unnamed x79 -> x0, local copies, waits for them, and re-layouts: 39.4 us -> none
    dot_general x11 -> x0, matrix products: 31.7 us -> none  [dot(): lax.dot_general(left, right, (dims, ((), ())), precision=lax.Precision.HI...]
    pallas_call x1 -> x2, Pallas kernels: 36.4 us -> 52.5 us  [the longest x1 38 us: joint_gram(): pl.pallas_call(functools.partial(reduce_kernel, n, chunk), out_shape=(jax...]
    transpose x11 -> x0, local copies, waits for them, and re-layouts: 13.3 us -> none  [the longest x10 12.1 us: tile(): return tile(j, i).T]
    gather x3 -> x0, local copies, waits for them, and re-layouts: 7.6 us -> none  [the longest x1 4.52 us: shards(): jnp.diagonal(raw_gram)]
    concatenate x5 -> x0, local copies, waits for them, and re-layouts: 3.25 us -> none  [the longest x3 2.52 us: unpack(): jnp.concatenate([tile(i, j) for j in range(tiles)], axis=1)]
    reduce_sum x3 -> x0, other arithmetic: 1.7 us -> none  [the longest x1 1.27 us: row_bound(): return jnp.max(jnp.sum(jnp.abs(matrix), axis=1))]
where the time goes in v2:
time: 54 us; the launch traced here: 53.8 us
  Pallas kernels  52.5 us (97%)
  between operations  1.28 us (2%)
    pallas_call x1, Pallas kernels, joint_gram(): pl.pallas_call(functools.partial(reduce_kernel, n, chunk), out_shape=(jax...  38 us
    pallas_call x1, Pallas kernels, update(): pl.pallas_call(update_kernel, out_shape=(jax.ShapeDtypeStruct((voxels, at...  14.5 us

profile of v2, /device:TPU:0, one launch (start us, length us, event | category | flops | bytes accessed | tf_op | source)
XLA Modules:
  0.0 53.8 jit_solution(9964952966934283247)
XLA Ops:
  1.3 38.0 %shard_map.76 = (f32[3,896,128]{2,1,0:T(8,128)}, bf16[768,768]{1,0:T(8,128)(2,1)}, bf16[768,768]{1,0:T(8,128)(2,1)}) custom-call(s32[1,256]{1,0:T(1,128)} %bitcast.2, f32[512,768]{1,0:T(8,128)} %vol_ref.1, f32[768,512]{1,0:T(8,128)} %dict_ref.1), custom_call_target="tpu_custom_call" | custom-call | tf_op jit(solution)/shard_map/pallas_call | solution.py:185
  39.3 14.5 %shard_map.77 = (f32[768,512]{1,0:T(8,128)}, f32[256,512]{1,0:T(8,128)}, f32[512,512]{1,0:T(8,128)}) custom-call(f32[3,896,128]{2,1,0:T(8,128)} %get-tuple-element.6.flat_ref, s32[1,256]{1,0:T(1,128)} %bitcast.3, s32[1,512]{1,0:T(1,128)} %bitcast.4, s32[1]{0:T(128)S(6)} %copy.8.held_ref, bf16[768,768]{1,0:T(8,128)(2,1)} %get-tuple-element.7.high_in, ...), custom_call_target="tpu_custom_call" | custom-call | tf_op jit(solution)/shard_map/pallas_call | solution.py:299

commit v3 on v2

--- a/solution.py
+++ b/solution.py
@@ -9,6 +9,7 @@
 
 ISTA_STEPS = 5
 PIECES = 3
+SLOPE = 8
 LANES = 128
 STRIP = 256
 
@@ -44,130 +45,158 @@
     return lax.broadcasted_iota(jnp.int32, (column.shape[0], records), 1) == column
 
 
+def sequence(atom_tiles, tiles):
+    within = [(i, j) for i, j in pairs(atom_tiles)]
+    across = [(i, j) for i in range(atom_tiles) for j in range(atom_tiles, tiles)]
+    return within + across + [(i, j) for i, j in pairs(tiles) if i >= atom_tiles]
+
+
+def bit_order(piece, bits):
+    order = list(range(bits))
+    if piece % 4 == 1:
+        order[1], order[2] = 2, 1
+    return order
+
+
 def reduce_kernel(
-    n, chunk, index_ref, vol_ref, dict_ref, out_ref, high_out, low_out,
-    joint_h, joint_l, turned_h, turned_l, x_ref, got0, sum0, got1, sum1, got2,
-    sem0, sem1, sem2, gat2, gat1, gat0, keep,
+    n, chunk, index_ref, vol_in, dict_in, out_ref, high_out, low_out,
+    vol_ref, dict_ref, joint_h, joint_l, turned_h, turned_l, x_ref, got, sems, keep,
 ):
     me = lax.axis_index("vox")
-    low, mid, high = lax.rem(me, 2), lax.rem(me // 2, 2), me // 4
-    peers = n // 4
-    half, quarter = n // 2 * chunk, n // 4 * chunk
-    mate0 = {"vox": me + 1 - 2 * low}
-    mate1 = {"vox": me + 2 - 4 * mid}
-    there = [lax.rem(high + step, peers) for step in range(1, peers)]
-    back = [lax.rem(high + peers - step, peers) for step in range(1, peers)]
+    bits = n.bit_length() - 1
+    bit = [lax.rem(me // 2 ** b, 2) for b in range(bits)]
+    mate = [{"vox": me + (1 - 2 * bit[b]) * 2 ** b} for b in range(bits)]
+    rows = n * chunk
+    loads = [
+        pltpu.make_async_copy(dict_in, dict_ref, keep.at[2]),
+        pltpu.make_async_copy(vol_in, vol_ref, keep.at[3]),
+    ]
+    for c in loads:
+        c.start()
+    barrier = pltpu.get_barrier_semaphore()
+    for to in mate:
+        pl.semaphore_signal(barrier, inc=1, device_id=to, device_id_type=MESH)
 
     def at(start, size):
         return pl.ds(pl.multiple_of(start, 8), size)
 
-    place = low * half + mid * quarter
-    own = at(place + high * chunk, chunk)
-
-    def device(z):
-        return {"vox": z * 4 + mid * 2 + low}
-
-    def copy(src, dst, sems, index, to):
-        return pltpu.make_async_remote_copy(
-            src_ref=src, dst_ref=dst, send_sem=sems.at[(0,) + index], recv_sem=sems.at[(1,) + index],
-            device_id=to, device_id_type=MESH,
+    starts = []
+    for k in range(PIECES):
+        start, path = 0, [0]
+        for s, b in enumerate(bit_order(k, bits)):
+            start = start + bit[b] * (rows >> (s + 1))
+            path.append(start)
+        starts.append(path)
+
+    copies = {}
+
+    def send(k, t):
+        gathers = t >= bits
+        s = 2 * bits - 1 - t if gathers else t
+        b = bit_order(k, bits)[s]
+        half = rows >> (s + 1)
+        if gathers:
+            src = dst = out_ref.at[k, at(starts[k][s + 1], half)]
+        else:
+            src = x_ref.at[k, at(starts[k][s] + (1 - bit[b]) * half, half)]
+            dst = got.at[k, pl.ds(rows - (rows >> s), half)]
+        c = pltpu.make_async_remote_copy(
+            src_ref=src, dst_ref=dst, send_sem=sems.at[0, t, k], recv_sem=sems.at[1, t, k],
+            device_id=mate[b], device_id_type=MESH,
         )
-
-    barrier = pltpu.get_barrier_semaphore()
-    for to in [mate0, mate1] + [device(z) for z in there]:
-        pl.semaphore_signal(barrier, inc=1, device_id=to, device_id_type=MESH)
+        c.start()
+        copies[(k, t)] = c
+
+    def advance(k, t):
+        if t <= bits:
+            copies[(k, t - 1)].wait_recv()
+            half = rows >> t
+            spot = at(starts[k][t], half)
+            value = x_ref[k, spot] + got[k, pl.ds(rows - (rows >> (t - 1)), half)]
+            if t == bits:
+                out_ref[k, spot] = value
+            else:
+                x_ref[k, spot] = value
+        else:
+            s = 2 * bits - t
+            b = bit_order(k, bits)[s]
+            half = rows >> (s + 1)
+            spot = out_ref.at[k, at(starts[k][s] + (1 - bit[b]) * half, half)]
+            pltpu.make_async_remote_copy(
+                src_ref=spot, dst_ref=spot, send_sem=sems.at[0, t - 1, k], recv_sem=sems.at[1, t - 1, k],
+                device_id=mate[b], device_id_type=MESH,
+            ).wait_recv()
+        if t < 2 * bits:
+            send(k, t)
 
     atoms = dict_ref.shape[1]
     size = joint_h.shape[1]
-    picked = jnp.where(match(index_ref, vol_ref.shape[0]), 1.0, 0.0).astype(jnp.bfloat16)
-    for part, joint, turned in zip(split(vol_ref[...]), (joint_h, joint_l), (turned_h, turned_l)):
-        rows = dot(picked, part).astype(jnp.bfloat16)
-        turned[atoms:] = rows
-        joint[:, atoms:] = rows.T
+    tiles = size // LANES
+    per_piece = rows // LANES
+    order = {pair: t for t, pair in enumerate(sequence(atoms // LANES, tiles))}
+    for t in range(len(order), PIECES * per_piece):
+        x_ref[t // per_piece, pl.ds(t % per_piece * LANES, LANES)] = jnp.zeros((LANES, LANES), jnp.float32)
+    stored = set()
+    begun = []
+    finished = set()
+
+    def store(top, left, strip):
+        for i in range(top // LANES, (top + strip.shape[0]) // LANES):
+            for j in range(max(i, left // LANES), (left + strip.shape[1]) // LANES):
+                t = order[(i, j)]
+                x_ref[t // per_piece, pl.ds(t % per_piece * LANES, LANES)] = strip[
+                    i * LANES - top:(i + 1) * LANES - top, j * LANES - left:(j + 1) * LANES - left
+                ]
+                stored.add(t)
+        for k in range(len(begun), PIECES):
+            if all(t in stored or t >= len(order) for t in range(k * per_piece, (k + 1) * per_piece)):
+                if k == 0:
+                    pl.semaphore_wait(barrier, bits)
+                begun.append(k)
+                send(k, 0)
+            else:
+                break
+
+    def gram(top, height, left, right):
+        store(top, left, dot3(
+            (turned_h[top:top + height], turned_l[top:top + height]),
+            (joint_h[:, left:right], joint_l[:, left:right]),
+        ))
+
+    def pump(steps):
+        for t in range(1, steps + 1):
+            for k in begun:
+                if (k, t) not in finished:
+                    finished.add((k, t))
+                    advance(k, t)
+
+    loads[0].wait()
     for part, joint, turned in zip(split(dict_ref[...]), (joint_h, joint_l), (turned_h, turned_l)):
         joint[:, :atoms] = part
         turned[:atoms] = part.T
+    for top in range(0, atoms, STRIP):
+        gram(top, STRIP, top, atoms)
+    loads[1].wait()
+    picked = jnp.where(match(index_ref, vol_ref.shape[0]), 1.0, 0.0).astype(jnp.bfloat16)
+    for part, joint, turned in zip(split(vol_ref[...]), (joint_h, joint_l), (turned_h, turned_l)):
+        picks = dot(picked, part).astype(jnp.bfloat16)
+        turned[atoms:] = picks
+        joint[:, atoms:] = picks.T
+    pump(1)
+    for top in range(0, atoms, STRIP):
+        gram(top, STRIP, atoms, size)
+        pump(1)
+    gram(atoms, size - atoms, atoms, size)
     saves = [
         pltpu.make_async_copy(joint_h, high_out, keep.at[0]),
         pltpu.make_async_copy(joint_l, low_out, keep.at[1]),
     ]
     for c in saves:
         c.start()
-
-    tiles = size // LANES
-    per_piece = n * chunk // LANES
-    order = {pair: t for t, pair in enumerate(pairs(tiles))}
-    for t in range(len(order), PIECES * per_piece):
-        x_ref[t // per_piece, pl.ds(t % per_piece * LANES, LANES)] = jnp.zeros((LANES, LANES), jnp.float32)
-    first = []
-
-    def send_first(k):
-        if k == 0:
-            pl.semaphore_wait(barrier, 2 + len(there))
-        c = copy(x_ref.at[k, at((1 - low) * half, half)], got0.at[k], sem0, (k,), mate0)
-        c.start()
-        first.append(c)
-
-    done = 0
-    for top in range(0, size, STRIP):
-        strip = dot3(
-            (turned_h[top:top + STRIP], turned_l[top:top + STRIP]), (joint_h[:, top:], joint_l[:, top:])
-        )
-        for i in range(top // LANES, (top + STRIP) // LANES):
-            for j in range(i, tiles):
-                t = order[(i, j)]
-                x_ref[t // per_piece, pl.ds(t % per_piece * LANES, LANES)] = strip[
-                    i * LANES - top:(i + 1) * LANES - top, j * LANES - top:(j + 1) * LANES - top
-                ]
-                done += 1
-        while len(first) < PIECES and (done >= (len(first) + 1) * per_piece or done == len(order)):
-            send_first(len(first))
-
-    sends = []
-    second = []
-    for k in range(PIECES):
-        first[k].wait_recv()
-        sum0[k] = x_ref[k, at(low * half, half)] + got0[k]
-        c = copy(sum0.at[k, at((1 - mid) * quarter, quarter)], got1.at[k], sem1, (k,), mate1)
-        c.start()
-        second.append(c)
-    third = []
-    for k in range(PIECES):
-        second[k].wait_recv()
-        sum1[k] = sum0[k, at(mid * quarter, quarter)] + got1[k]
-        for step, z in enumerate(there):
-            c = copy(sum1.at[k, at(z * chunk, chunk)], got2.at[k, step], sem2, (k, step), device(z))
-            c.start()
-            third.append(c)
-    for k in range(PIECES):
-        total = sum1[k, at(high * chunk, chunk)]
-        for step in range(peers - 1):
-            third[k * (peers - 1) + step].wait_recv()
-            total = total + got2[k, step]
-        out_ref[k, own] = total
-        for step, z in enumerate(there):
-            c = copy(out_ref.at[k, own], out_ref.at[k, own], gat2, (k, step), device(z))
-            c.start()
-            sends.append(c)
-    for k in range(PIECES):
-        for step, z in enumerate(back):
-            spot = out_ref.at[k, at(place + z * chunk, chunk)]
-            copy(spot, spot, gat2, (k, step), device(z)).wait_recv()
-        spot = out_ref.at[k, at(place, quarter)]
-        c = copy(spot, spot, gat1, (k,), mate1)
-        c.start()
-        sends.append(c)
-    for k in range(PIECES):
-        spot = out_ref.at[k, at(low * half + (1 - mid) * quarter, quarter)]
-        copy(spot, spot, gat1, (k,), mate1).wait_recv()
-        spot = out_ref.at[k, at(low * half, half)]
-        c = copy(spot, spot, gat0, (k,), mate0)
-        c.start()
-        sends.append(c)
-    for k in range(PIECES):
-        spot = out_ref.at[k, at((1 - low) * half, half)]
-        copy(spot, spot, gat0, (k,), mate0).wait_recv()
-    for c in first + second + third + sends:
+    tasks = [(k, t) for k in range(PIECES) for t in range(1, 2 * bits + 1) if (k, t) not in finished]
+    for k, t in sorted(tasks, key=lambda task: (task[0] + SLOPE * task[1], -task[1])):
+        advance(k, t)
+    for c in copies.values():
         c.wait_send()
     for c in saves:
         c.wait()
@@ -178,7 +207,7 @@
     size = atoms + record_index.shape[1]
     rows = len(pairs(size // LANES)) * LANES
     chunk = -(-rows // (PIECES * n * 8)) * 8
-    peers = n // 4
+    bits = n.bit_length() - 1
     sem = pltpu.SemaphoreType.DMA
     vmem = pl.BlockSpec(memory_space=pltpu.VMEM)
     anywhere = pl.BlockSpec(memory_space=pl.ANY)
@@ -189,22 +218,19 @@
             jax.ShapeDtypeStruct((voxels, size), jnp.bfloat16),
             jax.ShapeDtypeStruct((voxels, size), jnp.bfloat16),
         ),
-        in_specs=[vmem] * 3,
+        in_specs=[vmem, anywhere, anywhere],
         out_specs=(vmem, anywhere, anywhere),
         scratch_shapes=[
+            pltpu.VMEM(volumes.shape, jnp.float32),
+            pltpu.VMEM(dictionary.shape, jnp.float32),
             pltpu.VMEM((voxels, size), jnp.bfloat16),
             pltpu.VMEM((voxels, size), jnp.bfloat16),
             pltpu.VMEM((size, voxels), jnp.bfloat16),
             pltpu.VMEM((size, voxels), jnp.bfloat16),
             pltpu.VMEM((PIECES, n * chunk, LANES), jnp.float32),
-            pltpu.VMEM((PIECES, n // 2 * chunk, LANES), jnp.float32),
-            pltpu.VMEM((PIECES, n // 2 * chunk, LANES), jnp.float32),
-            pltpu.VMEM((PIECES, n // 4 * chunk, LANES), jnp.float32),
-            pltpu.VMEM((PIECES, n // 4 * chunk, LANES), jnp.float32),
-            pltpu.VMEM((PIECES, peers, chunk, LANES), jnp.float32),
-            sem((2, PIECES)), sem((2, PIECES)), sem((2, PIECES, peers)),
-            sem((2, PIECES, peers)), sem((2, PIECES)), sem((2, PIECES)),
-            sem((2,)),
+            pltpu.VMEM((PIECES, n * chunk, LANES), jnp.float32),
+            sem((2, 2 * bits, PIECES)),
+            sem((4,)),
         ],
         compiler_params=pltpu.CompilerParams(collective_id=0, has_side_effects=True),
     )(record_index, volumes, dictionary)
@@ -224,7 +250,7 @@
     for c in loads:
         c.start()
     per_piece = flat_ref.shape[1] // LANES
-    for t, (i, j) in enumerate(pairs(size // LANES)):
+    for t, (i, j) in enumerate(sequence(atoms // LANES, size // LANES)):
         tile = flat_ref[t // per_piece, pl.ds(t % per_piece * LANES, LANES)]
         spots = [(i, j, tile)] + ([(j, i, tile.T)] if j > i else [])
         for row, column, value in spots:

time: 54 us -> 52.4 us (0.970)
  Pallas kernels: 52.5 us -> 50.9 us
    pallas_call x1, Pallas kernels: 38 us -> 36.4 us  [joint_gram(): pl.pallas_call(functools.partial(reduce_kernel, n, chunk), out_shape=(jax...]
where the time goes in v3:
time: 52.4 us; the launch traced here: 52.2 us
  Pallas kernels  50.9 us (97%)
  between operations  1.28 us (2%)
    pallas_call x1, Pallas kernels, joint_gram(): pl.pallas_call(functools.partial(reduce_kernel, n, chunk), out_shape=(jax...  36.4 us
    pallas_call x1, Pallas kernels, update(): pl.pallas_call(update_kernel, out_shape=(jax.ShapeDtypeStruct((voxels, at...  14.5 us

profile of v3, /device:TPU:0, one launch (start us, length us, event | category | flops | bytes accessed | tf_op | source)
XLA Modules:
  0.0 52.2 jit_solution(14211016377764575030)
XLA Ops:
  1.3 36.4 %shard_map.76 = (f32[3,896,128]{2,1,0:T(8,128)}, bf16[768,768]{1,0:T(8,128)(2,1)}, bf16[768,768]{1,0:T(8,128)(2,1)}) custom-call(s32[1,256]{1,0:T(1,128)} %bitcast.2, f32[512,768]{1,0:T(8,128)} %vol_in.1, f32[768,512]{1,0:T(8,128)} %dict_in.1), custom_call_target="tpu_custom_call" | custom-call | tf_op jit(solution)/shard_map/pallas_call | solution.py:214
  37.6 14.5 %shard_map.77 = (f32[768,512]{1,0:T(8,128)}, f32[256,512]{1,0:T(8,128)}, f32[512,512]{1,0:T(8,128)}) custom-call(f32[3,896,128]{2,1,0:T(8,128)} %get-tuple-element.6.flat_ref, s32[1,256]{1,0:T(1,128)} %bitcast.3, s32[1,512]{1,0:T(1,128)} %bitcast.4, s32[1]{0:T(128)S(6)} %copy.8.held_ref, bf16[768,768]{1,0:T(8,128)(2,1)} %get-tuple-element.7.high_in, ...), custom_call_target="tpu_custom_call" | custom-call | tf_op jit(solution)/shard_map/pallas_call | solution.py:325
